TPU v7x, 32 devices: a whole 2x2x4 slice. The times are simulated.
32 devices in a mesh: group: 2 (over y), ctx: 4 (over z), head: 4 (over x, core).
Axes of the slice: x: 2, y: 2, z: 4, core: 2. Of those that a mesh axis runs over, the one named last changes fastest.
Arguments:
- mixer_x: bfloat16 [2048, 8192], P(('group', 'ctx'), 'head'), parts along dimension 0, may hold values from -6 to 6
- mixer_bc: bfloat16 [2, 2048, 1024], P(None, ('group', 'ctx'), 'head'), parts along dimension 1, may hold values from -3 to 3
- mixer_gate: bfloat16 [2048, 8192], P(('group', 'ctx'), 'head'), parts along dimension 0, may hold values from -9 to 9
- step_logits: float32 [2048, 128], P(('group', 'ctx'), 'head'), parts along dimension 0, may hold values from -3 to 3
- conv_x_weight: float32 [4, 8192], P(None, 'head'), may hold values from -0.6 to 0.6
- conv_bc_weight: float32 [2, 4, 1024], P(None, None, 'head'), may hold values from -0.6 to 0.6
- head_params: float32 [3, 128], P(None, 'head'), as said below
- norm_gain: float32 [8192], P('head'), may hold values from 0.5 to 1.5
- grad_output: bfloat16 [2048, 8192], P(('group', 'ctx'), 'head'), parts along dimension 0, may hold values from -9 to 9
Outputs:
- grad_x: bfloat16 [2048, 8192], P(('group', 'ctx'), 'head'), parts along dimension 0
- grad_bc: bfloat16 [2, 2048, 1024], P(None, ('group', 'ctx'), 'head'), parts along dimension 1
- grad_gate: bfloat16 [2048, 8192], P(('group', 'ctx'), 'head'), parts along dimension 0
- grad_step: float32 [2048, 128], P(('group', 'ctx'), 'head'), parts along dimension 0
- grad_conv_x: float32 [8, 8192], P('group', 'head'), parts along dimension 0
- grad_conv_bc: float32 [4, 4, 1024], P('group', None, 'head'), parts along dimension 0
- grad_heads: float32 [6, 128], P('group', 'head'), parts along dimension 0
- grad_gain: float32 [16384], P(('group', 'head')), parts along dimension 0
There are 2 independent parts, one for each index of `group`. A program takes and returns all parts, laid end to end along the dimension named above; an argument that names none is the same for every part. Nothing has to cross between parts.
Inputs may be any that keep to these rules, and one draw needn't show every extreme that they name: `head_params`: row 0 is added to the step logits and lies between -1 and 1; row 1 is the logarithm of a decay rate between log(0.2 / 1024) and log(0.1); row 2 is a skip factor between 0.5 and 1.5.
All inputs are finite; a program needn't handle non-finite values.
Results may differ from a plain program's by a relative error of at most 0.014.
Values may be sent and summed in bfloat16 or wider, within the bound.
A program may use at most 128 MiB of HBM per device.

v0:
```python
import jax
import jax.numpy as jnp
from jax import lax
from jax.sharding import PartitionSpec as P

HEADS = 128
HEAD_DIM = 64
STATE = 128
GROUPS = 8
CONV = 4
SPAN = 256
INNER = 8192


epsilon = 1e-05


def passed_along(shard, axis, by):
    size = lax.axis_size(axis)
    pairs = [(i, i + by) for i in range(size) if 0 <= i + by < size]
    return lax.ppermute(shard, axis, pairs)


def entering_2(shard, axis, combine, identity):
    size, position = (lax.axis_size(axis), lax.axis_index(axis))
    everything = jax.tree.map(
        lambda part, kind: lax.all_gather(part.astype(kind), axis),
        shard,
        (jnp.bfloat16, jnp.bfloat16),
    )
    start = jax.tree.map(
        lambda part, zero: jnp.broadcast_to(jnp.asarray(zero, part.dtype), part.shape),
        shard,
        identity,
    )

    def entering_step(k, before):
        reached = k < position
        new = combine(
            before, jax.tree.map(lambda part, own: part[k].astype(own.dtype), everything, shard)
        )
        return jax.tree.map(lambda a, b: jnp.where(reached, a, b), new, before)

    return lax.fori_loop(0, size, entering_step, start)


def prefix(shard, axis, combine, identity):
    size, position = (lax.axis_size(axis), lax.axis_index(axis))
    everything = jax.tree.map(
        lambda part, kind: lax.all_gather(part.astype(kind), axis),
        shard,
        jax.tree.map(lambda a: jnp.bfloat16 if a.dtype == jnp.float32 else a.dtype, shard),
    )
    start = jax.tree.map(
        lambda part, zero: jnp.broadcast_to(jnp.asarray(zero, part.dtype), part.shape),
        shard,
        identity,
    )

    def prefix_step(k, before):
        at = size - 1 - k
        reached = at > position
        new = combine(
            before, jax.tree.map(lambda part, own: part[at].astype(own.dtype), everything, shard)
        )
        return jax.tree.map(lambda a, b: jnp.where(reached, a, b), new, before)

    return lax.fori_loop(0, size, prefix_step, start)


def conv_silu(padded_rows, kernel):
    taps_count = kernel.shape[0]
    out_rows = padded_rows.shape[0] - taps_count + 1
    summed = kernel[0] * padded_rows[0:out_rows]
    for offset in range(1, taps_count):
        summed = summed + kernel[offset] * padded_rows[offset : offset + out_rows]
    return jax.nn.silu(summed).astype(jnp.bfloat16)


def span_parts(x_block, b_block, c_block, step_block, decay_rate, skip_gain):
    log_decay = jnp.cumsum(step_block * decay_rate, axis=0)
    block_end = log_decay[-1]
    scores = jnp.einsum("tgn,sgn->gts", c_block, b_block, preferred_element_type=jnp.float32)
    by_head = jnp.transpose(log_decay, (1, 2, 0))
    spread = by_head[:, :, :, None] - by_head[:, :, None, :]
    positions = jnp.arange(log_decay.shape[0])
    causal = positions[:, None] >= positions[None, :]
    weights = jnp.where(causal, jnp.exp(jnp.where(causal, spread, 0.0)), 0.0)
    step_heads = jnp.transpose(step_block, (1, 2, 0))
    mixing = (scores[:, None] * weights * step_heads[:, :, None, :]).astype(jnp.bfloat16)
    inside = jnp.einsum("gkts,sgkp->tgkp", mixing, x_block, preferred_element_type=jnp.float32)
    inside = inside + skip_gain[None, :, :, None] * x_block.astype(jnp.float32)
    carry_weight = jnp.exp(block_end[None] - log_decay) * step_block
    scaled_x = (x_block.astype(jnp.float32) * carry_weight[..., None]).astype(jnp.bfloat16)
    block_state = jnp.einsum(
        "sgkp,sgn->gkpn", scaled_x, b_block, preferred_element_type=jnp.float32
    )
    return (inside, block_state, block_end, log_decay)


def state_read(c_block, state_low, log_decay):
    readout = jnp.einsum("tgn,gkpn->tgkp", c_block, state_low, preferred_element_type=jnp.float32)
    return readout * jnp.exp(log_decay)[..., None]


def join_states(earlier, later):
    return (earlier[0] + later[0], jnp.exp(later[0])[..., None, None] * earlier[1] + later[1])


def shards(
    mixer_x,
    mixer_bc,
    mixer_gate,
    step_logits,
    conv_x_weight,
    conv_bc_weight,
    head_params,
    norm_gain,
    grad_output,
):
    margin = CONV - 1
    length_dev = mixer_x.shape[0]
    width_dev = mixer_x.shape[1]
    columns = mixer_bc.shape[2]
    groups = columns // STATE
    per_group = HEADS // GROUPS
    blocks = length_dev // SPAN
    rim_rows = jnp.concatenate(
        [
            mixer_x[length_dev - margin :],
            mixer_bc[0, length_dev - margin :],
            mixer_bc[1, length_dev - margin :],
        ],
        axis=1,
    )
    before = passed_along(rim_rows, "ctx", 1)

    def prepare(x_own, bc_own, borrowed, step_own, conv_x, conv_bc, params_own):
        x_rows = jnp.concatenate([borrowed[:, :width_dev], x_own], axis=0)
        b_rows = jnp.concatenate([borrowed[:, width_dev : width_dev + columns], bc_own[0]], axis=0)
        c_rows = jnp.concatenate([borrowed[:, width_dev + columns :], bc_own[1]], axis=0)
        x_conv = conv_silu(x_rows, conv_x)
        b_conv = conv_silu(b_rows, conv_bc[0])
        c_conv = conv_silu(c_rows, conv_bc[1])
        step_size = jax.nn.softplus(step_own + params_own[0])
        decay_rate = (-jnp.exp(params_own[1])).reshape(groups, per_group)
        skip_gain = params_own[2].reshape(groups, per_group)
        x_blocks = x_conv.reshape(blocks, SPAN, groups, per_group, HEAD_DIM)
        b_blocks = b_conv.reshape(blocks, SPAN, groups, STATE)
        c_blocks = c_conv.reshape(blocks, SPAN, groups, STATE)
        step_blocks = step_size.reshape(blocks, SPAN, groups, per_group)
        inside_all, block_states, block_ends, log_decays = jax.vmap(
            span_parts, in_axes=(0, 0, 0, 0, None, None)
        )(x_blocks, b_blocks, c_blocks, step_blocks, decay_rate, skip_gain)
        return (inside_all, block_states, block_ends, log_decays, c_blocks)

    primals = (
        mixer_x.astype(jnp.float32),
        mixer_bc.astype(jnp.float32),
        before.astype(jnp.float32),
        step_logits,
        conv_x_weight,
        conv_bc_weight,
        head_params,
    )
    prepared, pull_prepare = jax.vjp(prepare, *primals)
    inside_all, block_states, block_ends, log_decays, c_blocks = prepared
    device_log = block_ends[0]
    device_state = block_states[0]
    empty_log = jnp.zeros_like(device_log)
    empty_state = jnp.zeros_like(device_state)
    halfway = per_group // 2
    lower_half = entering_2(
        (device_log[:, :halfway], device_state[:, :halfway]),
        "ctx",
        join_states,
        (empty_log[:, :halfway], empty_state[:, :halfway]),
    )
    upper_half = entering_2(
        (device_log[:, halfway:], device_state[:, halfway:]),
        "ctx",
        join_states,
        (empty_log[:, halfway:], empty_state[:, halfway:]),
    )
    carried = jnp.concatenate([lower_half[1], upper_half[1]], axis=1)
    number = 0
    entering = [carried]
    entering_low = jnp.stack(entering).astype(jnp.bfloat16)

    def read_all(c_part, state_part, decay_part):
        return jax.vmap(state_read)(c_part, state_part, decay_part)

    readouts, pull_read = jax.vjp(read_all, c_blocks, entering_low, log_decays)
    mixed = (inside_all + readouts).reshape(length_dev, width_dev)
    gate_value = mixer_gate.astype(jnp.float32)
    sigmoid_z = jax.nn.sigmoid(gate_value)
    gate_act = gate_value * sigmoid_z
    gated = mixed * gate_act
    upstream = grad_output.astype(jnp.float32) * norm_gain
    own_square = jnp.sum(gated * gated, axis=1)
    square = lax.psum(own_square, "head")
    factor = lax.rsqrt(square / INNER + epsilon)
    normed = gated * factor[:, None]
    projected = lax.psum(jnp.sum(upstream * normed, axis=1), "head")
    d_gated = (upstream - normed * (projected / INNER)[:, None]) * factor[:, None]
    grad_gain_own = jnp.sum(grad_output.astype(jnp.float32) * normed, axis=0)
    d_mixed = d_gated * gate_act
    grad_gate = (d_gated * mixed * (sigmoid_z * (1.0 + gate_value * (1.0 - sigmoid_z)))).astype(
        jnp.bfloat16
    )
    grad_blocks = d_mixed.reshape(inside_all.shape)
    d_c_read, d_entering_low, d_decay_read = pull_read(grad_blocks)
    d_entering = d_entering_low.astype(jnp.float32)
    pending = jnp.zeros_like(carried)
    after_zero = [None] * blocks
    for number in reversed(range(blocks)):
        after_zero[number] = pending
        pending = d_entering[number] + jnp.exp(block_ends[number])[..., None, None] * pending
    outgoing = prefix((device_log, pending), "ctx", join_states, (empty_log, empty_state))[1]
    decay_after = jnp.zeros_like(device_log)
    grad_states = [None] * blocks
    grad_ends = [None] * blocks
    for number in reversed(range(blocks)):
        state_grad = after_zero[number] + jnp.exp(decay_after)[..., None, None] * outgoing
        grad_states[number] = state_grad
        grad_ends[number] = jnp.exp(block_ends[number]) * jnp.sum(
            state_grad * entering[number], axis=(2, 3)
        )
        decay_after = block_ends[number]
    gradients = pull_prepare(
        (grad_blocks, jnp.stack(grad_states), jnp.stack(grad_ends), d_decay_read, d_c_read)
    )
    returned = passed_along(gradients[2], "ctx", -1)
    grad_x = (
        gradients[0].at[length_dev - margin :].add(returned[:, :width_dev]).astype(jnp.bfloat16)
    )
    grad_b = (
        gradients[1][0].at[length_dev - margin :].add(returned[:, width_dev : width_dev + columns])
    )
    grad_c = gradients[1][1].at[length_dev - margin :].add(returned[:, width_dev + columns :])
    grad_bc = jnp.stack([grad_b, grad_c]).astype(jnp.bfloat16)
    totals = lax.psum((gradients[4], gradients[5], gradients[6], grad_gain_own), "ctx")
    return (grad_x, grad_bc, grad_gate, gradients[3], totals[0], totals[1], totals[2], totals[3])


def solution(mesh):
    return jax.shard_map(
        shards,
        mesh=mesh,
        in_specs=(
            P(("group", "ctx"), "head"),
            P(None, ("group", "ctx"), "head"),
            P(("group", "ctx"), "head"),
            P(("group", "ctx"), "head"),
            P(None, "head"),
            P(None, None, "head"),
            P(None, "head"),
            P("head"),
            P(("group", "ctx"), "head"),
        ),
        out_specs=(
            P(("group", "ctx"), "head"),
            P(None, ("group", "ctx"), "head"),
            P(("group", "ctx"), "head"),
            P(("group", "ctx"), "head"),
            P("group", "head"),
            P("group", None, "head"),
            P("group", "head"),
            P(("group", "head")),
        ),
        check_vma=False,
    )
```

profile of v0, /device:TPU:0, one launch (start us, length us, event | category | flops | bytes accessed | tf_op | source)
XLA Modules:
  0.0 249.9 jit_solution(2895747203639951558)
XLA Ops:
  8.7 5.0 %collective-permute-start = (bf16[3,2560]{1,0:T(4,128)(2,1)S(1)}, bf16[3,2560]{1,0:T(4,128)(2,1)S(1)}, u32[]{:S(2)}, u32[]{:S(2)}) collective-permute-start(bf16[3,2560]{1,0:T(4,128)(2,1)S(1)} %pad_maximum_fusion.4), channel_id=1, source_target_pairs={{0,4},{4,8},{8,12},{1,5},{5,9},{9,13},{2,6},{6,10},{10,14},{3,7},{... | collective-permute-start | bytes 46088 | tf_op jit(solution)/shard_map/ppermute | solution.py:21
  27.2 6.4 %multiply_convert_fusion.5 = (bf16[256,2048]{0,1:T(8,128)(2,1)S(1)}, f32[256,2048]{0,1:T(8,128)}) fusion(f32[256,2048]{0,1:T(8,128)S(1)} %convert_element_type.286, f32[2048]{0:T(1024)S(1)} %bitcast.392, f32[3,2048]{0,1:T(8,128)} %copy.222, f32[2048]{0:T(1024)S(1)} %bitcast.394, f32[2048]{0:T(1024)S(1)} %bitcast.396, f32[2048]{0:T(1024)S(1)} %bitcast.390), kind=kLoop, calls=%fused_computation.81 | loop fusion | flops 7864320 | bytes 5300224 | tf_op jit(solution)/shard_map/jvp()/convert_element_type | solution.py:77
  33.7 1.7 multiply_convert_fusion.16
  37.4 9.1 %all-gather.7 = bf16[4,2,8]{2,1,0:T(2,128)(2,1)S(1)} all-gather(bf16[1,2,8]{2,1,0:T(2,128)(2,1)S(1)} %get-tuple-element.588), channel_id=5, replica_groups=mesh['group'=2,'ctx'=4,'head'=4] {'ctx'}, dimensions={0}, use_global_device_ids=true | all-gather | bytes 160 | tf_op jit(solution)/shard_map/all_gather | solution.py:27
  46.5 8.5 %all-gather.6 = bf16[4,2,8]{2,1,0:T(2,128)(2,1)S(1)} all-gather(bf16[1,2,8]{2,1,0:T(2,128)(2,1)S(1)} %get-tuple-element.589), channel_id=3, replica_groups=mesh['group'=2,'ctx'=4,'head'=4] {'ctx'}, dimensions={0}, use_global_device_ids=true | all-gather | bytes 160 | tf_op jit(solution)/shard_map/all_gather | solution.py:27
  57.1 2.3 copy.235
  59.4 2.3 copy.220
  65.1 4.5 %while.48 = (s32[]{:T(128)}, f32[2,8,64,128]{3,2,1,0:T(8,128)S(1)}, s32[]{:T(128)}, bf16[4,2,8]{2,1,0:T(2,128)(2,1)S(1)}, bf16[4,2,8,64,128]{4,3,2,1,0:T(8,128)(2,1)}, /*index=5*/s32[]{:T(128)}, s32[]{:T(128)}) while((s32[]{:T(128)}, f32[2,8,64,128]{3,2,1,0:T(8,128)S(1)}, s32[]{:T(128)}, bf16[4,2,8]{2,1,0:T(2,128)(2,1)S(1)}, ...), condition=%wide.region_5.6_spmd.clone, body=%wide.region_4.5_spmd.clone.sunk | while | flops 655380 | bytes 1310985 | solution.py:44
  69.6 24.5 %all-gather.12.cloned.1.call-done = bf16[8,8,64,128]{3,2,1,0:T(8,128)(2,1)} async-done(((bf16[2,8,64,128]{3,2,1,0:T(8,128)(2,1)}), bf16[8,8,64,128]{3,2,1,0:T(8,128)(2,1)}) %all-gather.12.cloned.1.call-update) | async-done | bytes 1048592 | tf_op jit(solution)/shard_map/all_gather | solution.py:27
  94.1 4.5 %while.47 = (s32[]{:T(128)}, f32[2,8,64,128]{3,2,1,0:T(8,128)S(1)}, s32[]{:T(128)}, bf16[4,2,8]{2,1,0:T(2,128)(2,1)S(1)}, bf16[4,2,8,64,128]{4,3,2,1,0:T(8,128)(2,1)}, /*index=5*/s32[]{:T(128)}, s32[]{:T(128)}) while((s32[]{:T(128)}, f32[2,8,64,128]{3,2,1,0:T(8,128)S(1)}, s32[]{:T(128)}, bf16[4,2,8]{2,1,0:T(2,128)(2,1)S(1)}, ...), condition=%wide.region_3.4_spmd.clone, body=%wide.region_2.3_spmd.clone.sunk | while | flops 655380 | bytes 1310985 | solution.py:44
  99.9 2.8 %fusion.32 = f32[1,256,2,16,64]{1,4,3,2,0:T(8,128)S(1)} fusion(f32[2,16,64,256]{3,2,1,0:T(8,128)S(1)} %fusion.95, bf16[256,2,16,64]{0,3,2,1:T(8,128)(2,1)S(1)} %bitcast.359, f32[2,16,256]{2,1,0:T(8,128)S(1)} %bitcast.386, f32[2,16,256]{2,1,0:T(8,128)S(1)} %copy-done.61, f32[2,256,256]{2,1,0:T(8,128)S(1)} %copy-done.42, pred[256,256]{1,0:T(8,128)(4,1)S(1)} %copy-done.58, ...), kind=kOutput, calls=%fused_computation.58 | convolution fusion | flops 283639808 | bytes 6979712 | tf_op jit(solution)/shard_map/jvp(vmap(gkts,sgkp->tgkp))/dot_general | solution.py:91
  104.0 6.7 %psum.42 = f32[256]{0:T(256)} all-reduce(f32[256]{0:T(256)} %multiply_reduce_fusion.5), channel_id=1, replica_groups=mesh['group'=2,'ctx'=4,'head'=4] {'head'}, use_global_device_ids=true, to_apply=%region_7.8 | all-reduce | flops 256 | bytes 2048 | tf_op jit(solution)/shard_map/psum | solution.py:201
  111.4 3.6 %fusion.20 = (f32[2048]{0:T(1024)}, f32[256]{0:T(256)}) fusion(bf16[256,2048]{0,1:T(8,128)(2,1)} %copy.220, f32[256]{0:T(256)S(1)} %add_rsqrt_fusion, bf16[256,2048]{0,1:T(8,128)(2,1)} %copy.235, f32[1,256,2,16,64]{1,4,3,2,0:T(8,128)S(1)} %fusion.32, f32[2048]{0:T(1024)} %param.28), kind=kLoop, calls=%fused_computation.44 | loop fusion | flops 6813440 | bytes 4212736 | tf_op jit(solution)/shard_map/reduce_sum | solution.py:206
  115.0 6.3 %psum.43 = f32[256]{0:T(256)S(1)} all-reduce(f32[256]{0:T(256)} %get-tuple-element.477), channel_id=1, replica_groups=mesh['group'=2,'ctx'=4,'head'=4] {'head'}, use_global_device_ids=true, to_apply=%region_9.10 | all-reduce | flops 256 | bytes 2048 | tf_op jit(solution)/shard_map/psum | solution.py:204
  121.3 4.9 %multiply_reduce_fusion = (f32[2048]{0:T(1024)}, f32[256,2048]{0,1:T(8,128)S(1)}, bf16[256,2048]{0,1:T(8,128)(2,1)}) fusion(bf16[256,2048]{0,1:T(8,128)(2,1)S(1)} %get-tuple-element.538, f32[256]{0:T(256)S(1)} %broadcast_multiply_fusion.13, f32[256]{0:T(256)} %copy-done.82, bf16[256,2048]{0,1:T(8,128)(2,1)} %copy.235, f32[1,256,2,16,64]{1,4,3,2,0:T(8,128)} %copy-done, ...), kind=kLoop, calls=%fused_computation.73 | loop fusion | flops 12056576 | bytes 8407040 | tf_op jit(solution)/shard_map/transpose(jvp(vmap()))/reduce_sum | solution.py:92
  127.4 9.9 %all-gather = bf16[4,1,2,16]{3,2,1,0:T(2,128)(2,1)} all-gather(bf16[1,1,2,16]{3,2,1,0:T(2,128)(2,1)} %get-tuple-element.567), channel_id=2, replica_groups=mesh['group'=2,'ctx'=4,'head'=4] {'ctx'}, dimensions={0}, use_global_device_ids=true | all-gather | bytes 320 | tf_op jit(solution)/shard_map/all_gather | solution.py:50
  137.4 2.6 %fusion.33 = f32[256,2,16]{0,2,1:T(8,128)} fusion(f32[1,256,2,16,64]{1,4,3,2,0:T(8,128)S(1)} %bitcast.353, f32[2,16,64,256]{3,2,1,0:T(8,128)} %copy-done.14), kind=kLoop, calls=%fused_computation.61 | loop fusion | flops 1040384 | bytes 4227072 | tf_op jit(solution)/shard_map/transpose(jvp(vmap()))/reduce_sum | solution.py:103
  141.6 8.2 %fusion.13 = (f32[2,16,256]{2,1,0:T(8,128)}, f32[2,16,256]{2,1,0:T(8,128)}, f32[2,16,256]{2,1,0:T(8,128)}, bf16[2,256,256]{2,1,0:T(8,128)(2,1)}) fusion(f32[2,16,256]{2,1,0:T(8,128)} %bitcast.385, f32[2,16,256]{2,1,0:T(8,128)} %copy.228, f32[2,256,256]{2,1,0:T(8,128)} %fusion.124, pred[256,256]{1,0:T(8,128)(4,1)} %iota_compare_fusion, ...), kind=kOutput, calls=%fused_computation.23 | convolution fusion | flops 301834240 | bytes 4161536 | tf_op jit(solution)/shard_map/transpose(jvp(vmap(gkts,sgkp->tgkp)))/dot_general | solution.py:91
  151.4 1.6 copy.248
  158.7 2.3 copy.258
  160.9 1.9 fusion.70
  165.4 6.9 %all-gather.16.cloned.1.call-done = bf16[8,16,64,128]{3,2,1,0:T(8,128)(2,1)} async-done(((bf16[2,16,64,128]{3,2,1,0:T(8,128)(2,1)}), bf16[8,16,64,128]{3,2,1,0:T(8,128)(2,1)}) %all-gather.16.cloned.1.call-update) | async-done | bytes 2097168 | tf_op jit(solution)/shard_map/all_gather | solution.py:50
  172.2 7.9 %while.49 = (s32[]{:T(128)}, f32[2,16,64,128]{3,2,1,0:T(8,128)S(1)}, s32[]{:T(128)}, bf16[4,2,16]{2,1,0:T(2,128)(2,1)}, bf16[4,2,16,64,128]{4,3,2,1,0:T(8,128)(2...) while((s32[]{:T(128)}, f32[2,16,64,128]{3,2,1,0:T(8,128)S(1)}, s32[]{:T(128)}, ...), condition=%wide.region_11.12_spmd.clone, body=%wide.region_10.11_spmd.clone.sunk | while | flops 1310760 | bytes 2621927 | solution.py:68
  180.2 2.1 multiply_reduce_fusion.6
  184.0 1.7 multiply_reduce_fusion.14
  189.2 3.3 %fusion.59 = bf16[1,256,2,16,64]{1,4,3,2,0:T(8,128)(2,1)S(1)} fusion(f32[2,16,64,256]{3,2,1,0:T(8,128)S(1)} %bitcast.356, f32[2,16,256]{2,1,0:T(8,128)S(1)} %bitcast.387, f32[2,16,256]{2,1,0:T(8,128)S(1)} %copy-done.62, f32[2,256,256]{2,1,0:T(8,128)S(1)} %copy-done.43, pred[256,256]{1,0:T(8,128)(4,1)S(1)} %copy-done.59, ...), kind=kOutput, calls=%fused_computation.96 | convolution fusion | flops 284688384 | bytes 6979712 | tf_op jit(solution)/shard_map/transpose(jvp(vmap(gkts,sgkp->tgkp)))/dot_general | solution.py:91
  192.5 4.1 %multiply_reduce_fusion.3 = (f32[2048]{0:T(1024)S(1)}, f32[2048]{0:T(1024)S(1)}, f32[2048]{0:T(1024)S(1)}, f32[2048]{0:T(1024)S(1)}, f32[256,2048]{0,1:T(8,128)S(1)}) fusion(f32[256,2048]{0,1:T(8,128)S(1)} %copy-done.2, f32[3,2048]{0,1:T(8,128)S(1)} %copy-done.10, bf16[256,2048]{0,1:T(8,128)(2,1)S(1)} %copy-done.9, f32[256,2048]{0,1:T(8,128)S(1)} %copy-done.13, ...), kind=kLoop, calls=%fused_computation.76 | loop fusion | flops 11526144 | bytes 8445952 | tf_op jit(solution)/shard_map/transpose(jvp())/reduce_sum | solution.py:76
  196.7 1.8 broadcast_multiply_fusion.3
  198.5 2.5 pad_add_fusion
  204.1 5.0 %reduce-window.16 = f32[1,16,2,2,128]{4,1,2,3,0:T(8,128)S(1)} reduce-window(f32[1,16,2,2,128]{4,1,2,3,0:T(8,128)S(1)} %copy.249, f32[]{:T(128)} %constant.188.clone.1), window={size=1x1x1x1x128 pad=0_0x0_0x0_0x0_0x0_127}, to_apply=%region_20.21 | reduce-window | flops 1040384 | bytes 65540 | tf_op jit(solution)/shard_map/reduce-window.2
  213.8 20.3 %all-reduce.35 = (f32[4,2048]{1,0:T(4,128)}, f32[2,4,256]{2,1,0:T(4,128)}, f32[3,32]{1,0:T(4,128)}, f32[2048]{0:T(1024)}) all-reduce(f32[4,2048]{1,0:T(4,128)S(1)} %pad_add_fusion.11, f32[2,4,256]{2,1,0:T(4,128)S(1)} %pad_add_fusion.12, f32[3,32]{1,0:T(4,128)S(1)} %pad_add_fusion.13, ...), channel_id=1, replica_groups=mesh['group'=2,'ctx'=4,'head'=4] {'ctx'}, use_global_device_ids=true, to_apply=%region_26.27 | all-reduce | flops 12384 | bytes 99072 | tf_op jit(solution)/shard_map/psum | solution.py:242
  238.3 3.6 %scatter-add.10 = bf16[256,2048]{0,1:T(8,128)(2,1)S(1)} dynamic-update-slice(bf16[256,2048]{0,1:T(8,128)(2,1)S(1)} %copy-done.17, bf16[3,2048]{0,1:T(8,128)(2,1)S(1)} %slice_add_fusion, s32[]{:T(128)} %constant.194.clone.1, s32[]{:T(128)} %constant.187.clone.1) | dynamic-update-slice | bytes 24580 | tf_op jit(solution)/shard_map/scatter-add | solution.py:235
  (348 shorter events, 72.4 us)
Async XLA Ops:
  7.2 57.9 %all-gather.14.cloned.1.call-start = ((), (), s32[]{:S(2)}) async-start(), calls=%async_computation.1 | async-start | bytes 1310720 | tf_op jit(solution)/shard_map/all_gather | solution.py:27
  8.7 15.2 %collective-permute-start = (bf16[3,2560]{1,0:T(4,128)(2,1)S(1)}, bf16[3,2560]{1,0:T(4,128)(2,1)S(1)}, u32[]{:S(2)}, u32[]{:S(2)}) collective-permute-start(bf16[3,2560]{1,0:T(4,128)(2,1)S(1)} %pad_maximum_fusion.4), channel_id=1, source_target_pairs={{0,4},{4,8},{8,12},{1,5},{5,9},{9,13},{2,6},{6,10},{10,14},{3,7},{... | collective-permute-start | bytes 46088 | tf_op jit(solution)/shard_map/ppermute | solution.py:21
  21.7 5.3 %copy-start.54 = (f32[1,2048]{1,0:T(1,128)}, f32[1,2048]{1,0:T(1,128)S(1)}, u32[]{:S(2)}) copy-start(f32[1,2048]{1,0:T(1,128)S(1)} %get-tuple-element.575) | copy-start | bytes 24580
  21.7 5.3 %copy-start.56 = (f32[1,2048]{1,0:T(1,128)}, f32[1,2048]{1,0:T(1,128)S(1)}, u32[]{:S(2)}) copy-start(f32[1,2048]{1,0:T(1,128)S(1)} %get-tuple-element.576) | copy-start | bytes 24580
  23.9 9.7 %copy-start.1 = (f32[256,2048]{0,1:T(8,128)}, f32[256,2048]{0,1:T(8,128)S(1)}, u32[]{:S(2)}) copy-start(f32[256,2048]{0,1:T(8,128)S(1)} %convert_element_type.286) | copy-start | bytes 6291460
  27.0 6.5 %copy-start.20 = (f32[256,256]{0,1:T(8,128)S(1)}, f32[256,256]{0,1:T(8,128)}, u32[]{:S(2)}) copy-start(f32[256,256]{0,1:T(8,128)} %get-tuple-element.555) | copy-start | bytes 786436
  27.0 6.5 %copy-start.22 = (f32[256,256]{0,1:T(8,128)S(1)}, f32[256,256]{0,1:T(8,128)}, u32[]{:S(2)}) copy-start(f32[256,256]{0,1:T(8,128)} %get-tuple-element.556) | copy-start | bytes 786436
  27.0 6.5 %copy-start.27 = (f32[3,256]{0,1:T(8,128)S(1)}, f32[3,256]{0,1:T(8,128)}, u32[]{:S(2)}) copy-start(f32[3,256]{0,1:T(8,128)} %copy.224) | copy-start | bytes 9220
  27.1 6.5 %copy-start.29 = (f32[3,256]{0,1:T(8,128)S(1)}, f32[3,256]{0,1:T(8,128)}, u32[]{:S(2)}) copy-start(f32[3,256]{0,1:T(8,128)} %copy.225) | copy-start | bytes 9220
  27.1 6.5 %copy-start.66 = (f32[1,1,256]{2,1,0:T(1,128)S(1)}, f32[1,1,256]{2,1,0:T(1,128)}, u32[]{:S(2)}) copy-start(f32[1,1,256]{2,1,0:T(1,128)} %get-tuple-element.579) | copy-start | bytes 3076
  27.1 6.5 %copy-start.68 = (f32[1,1,256]{2,1,0:T(1,128)S(1)}, f32[1,1,256]{2,1,0:T(1,128)}, u32[]{:S(2)}) copy-start(f32[1,1,256]{2,1,0:T(1,128)} %get-tuple-element.580) | copy-start | bytes 3076
  27.1 6.5 %copy-start.70 = (f32[1,1,256]{2,1,0:T(1,128)S(1)}, f32[1,1,256]{2,1,0:T(1,128)}, u32[]{:S(2)}) copy-start(f32[1,1,256]{2,1,0:T(1,128)} %get-tuple-element.585) | copy-start | bytes 3076
  27.1 6.5 %copy-start.72 = (f32[1,1,256]{2,1,0:T(1,128)S(1)}, f32[1,1,256]{2,1,0:T(1,128)}, u32[]{:S(2)}) copy-start(f32[1,1,256]{2,1,0:T(1,128)} %get-tuple-element.586) | copy-start | bytes 3076
  27.1 6.5 %copy-start.74 = (f32[1,1,256]{2,1,0:T(1,128)S(1)}, f32[1,1,256]{2,1,0:T(1,128)}, u32[]{:S(2)}) copy-start(f32[1,1,256]{2,1,0:T(1,128)} %get-tuple-element.581) | copy-start | bytes 3076
  27.1 6.5 %copy-start.76 = (f32[1,1,256]{2,1,0:T(1,128)S(1)}, f32[1,1,256]{2,1,0:T(1,128)}, u32[]{:S(2)}) copy-start(f32[1,1,256]{2,1,0:T(1,128)} %get-tuple-element.582) | copy-start | bytes 3076
  27.1 6.5 %copy-start.78 = (f32[1,1,256]{2,1,0:T(1,128)S(1)}, f32[1,1,256]{2,1,0:T(1,128)}, u32[]{:S(2)}) copy-start(f32[1,1,256]{2,1,0:T(1,128)} %get-tuple-element.583) | copy-start | bytes 3076
  27.1 6.5 %copy-start.80 = (f32[1,1,256]{2,1,0:T(1,128)S(1)}, f32[1,1,256]{2,1,0:T(1,128)}, u32[]{:S(2)}) copy-start(f32[1,1,256]{2,1,0:T(1,128)} %get-tuple-element.584) | copy-start | bytes 3076
  27.2 8.3 %copy-start.47 = (f32[256,2,16]{0,2,1:T(8,128)S(1)}, f32[256,2,16]{0,2,1:T(8,128)}, u32[]{:S(2)}) copy-start(f32[256,2,16]{0,2,1:T(8,128)} %copy.231) | copy-start | bytes 98308
  33.6 87.7 %copy-start.3 = (bf16[256,2048]{0,1:T(8,128)(2,1)}, bf16[256,2048]{0,1:T(8,128)(2,1)S(1)}, u32[]{:S(2)}) copy-start(bf16[256,2048]{0,1:T(8,128)(2,1)S(1)} %get-tuple-element.538) | copy-start | bytes 3145732
  35.4 27.5 %copy-start.24 = (bf16[256,256]{0,1:T(8,128)(2,1)}, bf16[256,256]{0,1:T(8,128)(2,1)S(1)}, u32[]{:S(2)}) copy-start(bf16[256,256]{0,1:T(8,128)(2,1)S(1)} %get-tuple-element.540) | copy-start | bytes 393220
  35.4 20.3 %copy-start.32 = (f32[256,2,16]{2,1,0:T(2,128)S(1)}, f32[256,2,16]{2,1,0:T(2,128)}, u32[]{:S(2)}) copy-start(f32[256,2,16]{2,1,0:T(2,128)} %get-tuple-element.536) | copy-start | bytes 98308
  35.4 21.0 %copy-start.99 = (f32[32]{0:T(128)S(1)}, f32[32]{0:T(128)}, u32[]{:S(2)}) copy-start(f32[32]{0:T(128)} %get-tuple-element.493) | copy-start | bytes 388
  36.7 57.4 %all-gather.12.cloned.1.call-start = ((), (), s32[]{:S(2)}) async-start(), calls=%async_computation | async-start | bytes 1310720 | tf_op jit(solution)/shard_map/all_gather | solution.py:27
  62.9 109.3 %all-gather.16.cloned.1.call-start = ((), (), s32[]{:S(2)}) async-start(), calls=%async_computation.2 | async-start | bytes 2621440 | tf_op jit(solution)/shard_map/all_gather | solution.py:50
  102.7 12.3 %copy-start = (f32[1,256,2,16,64]{1,4,3,2,0:T(8,128)}, f32[1,256,2,16,64]{1,4,3,2,0:T(8,128)S(1)}, u32[]{:S(2)}) copy-start(f32[1,256,2,16,64]{1,4,3,2,0:T(8,128)S(1)} %fusion.32) | copy-start | bytes 6291460
  203.0 6.5 %copy-start.34 = (f32[2,16,256]{1,0,2:T(2,128)S(1)}, f32[2,16,256]{1,0,2:T(2,128)}, u32[]{:S(2)}) copy-start(f32[2,16,256]{1,0,2:T(2,128)} %copy.244) | copy-start | bytes 98308
  203.0 6.5 %copy-start.97 = (f32[2,16]{1,0:T(2,128)S(1)}, f32[2,16]{1,0:T(2,128)}, u32[]{:S(2)}) copy-start(f32[2,16]{1,0:T(2,128)} %copy-done.96) | copy-start | bytes 388
  203.5 6.5 %copy-start.50 = (f32[256,32]{0,1:T(8,128)S(1)}, f32[256,32]{0,1:T(8,128)}, u32[]{:S(2)}) copy-start(f32[256,32]{0,1:T(8,128)} %param.24) | copy-start | bytes 98308
  203.5 6.5 %copy-start.85 = (f32[32]{0:T(128)S(1)}, f32[32]{0:T(128)}, u32[]{:S(2)}) copy-start(f32[32]{0:T(128)} %copy-done.84) | copy-start | bytes 388
  203.5 8.2 %slice-start = ((f32[259,2048]{0,1:T(8,128)}), f32[3,2048]{0,1:T(8,128)S(1)}, s32[]{:S(2)}) async-start(f32[259,2048]{0,1:T(8,128)} %copy-done.7), calls=%async_computation.3 | async-start | bytes 2097152 | tf_op jit(solution)/shard_map/transpose(jvp())/split | solution.py:139
  203.5 8.2 %copy-start.41 = (f32[3,256]{0,1:T(8,128)S(1)}, f32[3,256]{0,1:T(8,128)}, u32[]{:S(2)}) copy-start(f32[3,256]{0,1:T(8,128)} %pad_add_fusion.9) | copy-start | bytes 9220
  212.2 21.9 %collective-permute-start.1 = (f32[3,2560]{1,0:T(4,128)S(1)}, f32[3,2560]{1,0:T(4,128)S(1)}, u32[]{:S(2)}, u32[]{:S(2)}) collective-permute-start(f32[3,2560]{1,0:T(4,128)S(1)} %copy.239), channel_id=1, source_target_pairs={{4,0},{8,4},{12,8},{5,1},{9,5},{13,9},{6,2},{10,6},{14,10},{7,3},{... | collective-permute-start | bytes 92168 | tf_op jit(solution)/shard_map/ppermute | solution.py:21
  (76 other events, 188.8 us)
Sparse Core Ops, SparseCore 0:
  36.8 28.2 all-gather.13
  66.7 27.3 all-gather.11
  127.6 44.6 all-gather.15
where the time goes:
time: 252 us; the launch traced here: 250 us
  other arithmetic  70 us (28%)
  blocking collectives  61 us (24%)
  local copies, waits for them, and re-layouts  41.1 us (16%)
  waiting for transfers between devices  32.5 us (13%)
  matrix products  23.3 us (9%)
  between operations  15.4 us (6%)
  starting transfers between devices  6.37 us (3%)
    all_gather x2, waiting for transfers between devices, entering_2(): lax.all_gather(part.astype(kind), axis)  25.6 us
    psum x1, blocking collectives, shards(): lax.psum((gradients[4], gradients[5], gradients[6], grad_gain_own), 'ctx')  20.3 us
    all_gather x2, blocking collectives, entering_2(): lax.all_gather(part.astype(kind), axis)  17.6 us
    dot_general x3, matrix products, span_parts(): jnp.einsum('gkts,sgkp->tgkp', mixing, x_block, preferred_element_type=jnp...  14.3 us
    unnamed x214, local copies, waits for them, and re-layouts  13.1 us
    all_gather x1, blocking collectives, prefix(): lax.all_gather(part.astype(kind), axis)  9.92 us
    select_n x8, other arithmetic, entering_step(): return jax.tree.map(lambda a, b: jnp.where(reached, a, b), new, before)  8.73 us
    convert_element_type x2, other arithmetic, conv_silu(): return jax.nn.silu(summed).astype(jnp.bfloat16)  8.12 us
  transfers between devices with their start and end apart: 5, of which 3 were waited for; matrix products, arithmetic and copies ran while one was open for 21% of the time, Pallas kernels for 0%

commit v1 on v0

v1 whole, which is shorter than its diff:
```python
import functools

import jax
import jax.numpy as jnp
from jax import lax
from jax.experimental import pallas as pl
from jax.experimental.pallas import tpu as pltpu
from jax.sharding import PartitionSpec as P

HEADS = 128
HEAD_DIM = 64
STATE = 128
GROUPS = 8
CONV = 4
SPAN = 256
INNER = 8192
PER_GROUP = HEADS // GROUPS
CHUNK = 256
HPC = CHUNK // HEAD_DIM
LOW = -1e30
epsilon = 1e-05

F32 = jnp.float32
BF16 = jnp.bfloat16
MESH = pl.DeviceIdType.MESH
HIGH = lax.Precision.HIGHEST


def dot(a, b, ca=1, cb=0, precision=None):
    return lax.dot_general(
        a, b, (((ca,), (cb,)), ((), ())), precision=precision, preferred_element_type=F32
    )


def sigmoid(v):
    return 1.0 / (1.0 + jnp.exp(-v))


def split_dot(a, sel):
    high = a.astype(BF16)
    low = (a - high.astype(F32)).astype(BF16)
    return dot(high, sel) + dot(low, sel)


def kernel(
    n_ctx, n_head,
    x_ref, bc_ref, gate_ref, logits_ref, wx_ref, wbc_ref, params_ref, gain_ref, go_ref,
    gx_ref, gbc_ref, ggate_ref, gstep_ref, gwx_ref, gwbc_ref, gparams_ref, ggain_ref,
    halo_x, halo_bc, cum_b, cum_p, step_p, cum_t, step_t, mask, tap, dtap,
    xc, pre_x, bcc, pre_bc, b_t, c_t, scores, mix, weight, scaled, added,
    f_recv, f_send, r_recv, r_send, mixed, d_mixed, acc_sq, acc_proj, stats,
    d_b, d_c, d_s, acc1, acc2, acc_row, border_send, border_recv, tail_x, tail_bc,
    part, totals,
    halo_s, halo_r, f_ss, f_rs, r_ss, r_rs, st_s, st_r, bo_s, bo_r, to_s, to_r,
):
    me = lax.axis_index("ctx")
    mh = lax.axis_index("head")
    T = x_ref.shape[0]
    width = x_ref.shape[1]
    columns = bc_ref.shape[2]
    groups = columns // STATE
    heads = width // HEAD_DIM
    chunks = width // CHUNK
    per_g = chunks // groups
    nxt = lax.rem(me + 1, n_ctx)
    prv = lax.rem(me + n_ctx - 1, n_ctx)

    barrier = pltpu.get_barrier_semaphore()
    for k in range(1, n_ctx):
        pl.semaphore_signal(
            barrier, inc=1, device_id={"ctx": lax.rem(me + k, n_ctx)}, device_id_type=MESH
        )
    for k in range(1, n_head):
        pl.semaphore_signal(
            barrier, inc=1, device_id={"head": lax.rem(mh + k, n_head)}, device_id_type=MESH
        )
    pl.semaphore_wait(barrier, n_ctx - 1 + n_head - 1)

    def remote(src, dst, s, r, **where):
        return pltpu.make_async_remote_copy(
            src_ref=src, dst_ref=dst, send_sem=s, recv_sem=r, device_id=where, device_id_type=MESH
        )

    halo_copies = [
        remote(x_ref.at[pl.ds(T - 16, 16), :], halo_x, halo_s.at[0], halo_r.at[0], ctx=nxt),
        remote(bc_ref.at[:, pl.ds(T - 16, 16), :], halo_bc, halo_s.at[1], halo_r.at[1], ctx=nxt),
    ]

    @pl.when(me < n_ctx - 1)
    def _():
        for c in halo_copies:
            c.start()

    shifted = logits_ref[...] + params_ref[0:1, :]
    step = jnp.maximum(shifted, 0.0) + jnp.log1p(jnp.exp(-jnp.abs(shifted)))
    rate = -jnp.exp(params_ref[1:2, :])
    rows = lax.broadcasted_iota(jnp.int32, (T, T), 0)
    cols = lax.broadcasted_iota(jnp.int32, (T, T), 1)
    lower = jnp.where(rows >= cols, 1.0, 0.0)
    mask[...] = jnp.where(rows >= cols, 0.0, LOW)
    cum = dot(lower, step * rate, precision=HIGH)
    cum_t[...] = jnp.transpose(cum)
    step_t[...] = jnp.transpose(step)
    half = lax.broadcasted_iota(jnp.int32, (T, 128), 1) < HEAD_DIM
    for h in range(heads):
        cum_b[h] = jnp.broadcast_to(cum[:, h : h + 1], (T, 128))
    for h in range(0, heads, 2):
        pair = slice((h // 2 % 2) * 128, (h // 2 % 2) * 128 + 128)
        cum_p[h // 4, :, pair] = jnp.where(half, cum_b[h], cum_b[h + 1])
        step_p[h // 4, :, pair] = jnp.where(
            half,
            jnp.broadcast_to(step[:, h : h + 1], (T, 128)),
            jnp.broadcast_to(step[:, h + 1 : h + 2], (T, 128)),
        )

    @pl.when(me > 0)
    def _():
        for c in halo_copies:
            c.wait_recv()

    @pl.when(me == 0)
    def _():
        halo_x[...] = jnp.zeros_like(halo_x)
        halo_bc[...] = jnp.zeros_like(halo_bc)

    @pl.when(me < n_ctx - 1)
    def _():
        for c in halo_copies:
            c.wait_send()

    def convolve(lanes, w):
        total = w[0:1] * tap[pl.ds(5, T), 0:lanes]
        for k in range(1, CONV):
            total = total + w[k : k + 1] * tap[pl.ds(5 + k, T), 0:lanes]
        return total

    for kind in range(2):
        for g in range(groups):
            at = slice(g * STATE, (g + 1) * STATE)
            tap[0:8, 0:STATE] = halo_bc[kind, :, at].astype(F32)[8:16]
            tap[8 : 8 + T, 0:STATE] = bc_ref[kind, :, at].astype(F32)
            pre = convolve(STATE, wbc_ref[kind, :, at])
            pre_bc[kind, g] = pre
            bcc[kind, g] = (pre * sigmoid(pre)).astype(BF16)
    for g in range(groups):
        b_t[g] = jnp.transpose(bcc[0, g].astype(F32)).astype(BF16)
        c_t[g] = jnp.transpose(bcc[1, g].astype(F32)).astype(BF16)
        scores[g] = dot(bcc[1, g], b_t[g])
        d_b[g] = jnp.zeros((T, STATE), F32)
        d_c[g] = jnp.zeros((T, STATE), F32)
        d_s[g] = jnp.zeros((T, T), F32)
    acc_sq[...] = jnp.zeros_like(acc_sq)
    acc_proj[...] = jnp.zeros_like(acc_proj)
    acc1[...] = jnp.zeros_like(acc1)
    acc2[...] = jnp.zeros_like(acc2)
    acc_row[...] = jnp.zeros_like(acc_row)
    part[...] = jnp.zeros_like(part)

    def span(c):
        return pl.ds(pl.multiple_of(c * CHUNK, CHUNK), CHUNK)

    sel_row = lax.broadcasted_iota(jnp.int32, (CHUNK, heads), 0) // HEAD_DIM
    sel_col = lax.broadcasted_iota(jnp.int32, (CHUNK, heads), 1)

    def selector(c):
        return jnp.where(sel_row + c * HPC == sel_col, 1.0, 0.0)

    def expand(c):
        return dot(params_ref[...], selector(c), ca=1, cb=1, precision=HIGH)[2:3]

    def forward_copy(c):
        return remote(f_send.at[c], f_recv.at[c], f_ss.at[c], f_rs.at[c], ctx=nxt)

    def reverse_copy(c):
        return remote(r_send.at[c], r_recv.at[c], r_ss.at[c], r_rs.at[c], ctx=prv)

    def prepare(c, carry):
        at = span(c)
        tap[0:8, :] = halo_x[:, at].astype(F32)[8:16]
        tap[8 : 8 + T, :] = x_ref[:, at].astype(F32)
        pre = convolve(CHUNK, wx_ref[:, at])
        pre_x[:, at] = pre
        x_low = (pre * sigmoid(pre)).astype(BF16)
        xc[:, at] = x_low
        cum_c = cum_p[c]
        carry_weight = jnp.exp(cum_c[T - 1 : T] - cum_c) * step_p[c]
        sc = (x_low.astype(F32) * carry_weight).astype(BF16)
        scaled[:, at] = sc
        added[:, at] = dot(b_t[c // per_g], sc)
        return carry

    def head_loop_forward(c):
        g = c // per_g
        base = scores[g]
        out = []
        for pair in range(HPC // 2):
            x_pair = xc[:, pl.ds(pl.multiple_of(c * CHUNK + pair * 128, 128), 128)]
            ys = []
            for q in range(2):
                h = c * HPC + pair * 2 + q
                col = cum_b[h]
                spread = jnp.concatenate([col, col], axis=1) - cum_t[pl.ds(h, 1), :] + mask[...]
                w = jnp.exp(spread) * step_t[pl.ds(h, 1), :]
                weight[h] = w
                m = (base * w).astype(BF16)
                mix[h] = m
                ys.append(dot(m, x_pair))
            out.append(jnp.where(half, ys[0], ys[1]))
        return jnp.concatenate(out, axis=1)

    def forward(c, carry):
        at = span(c)
        g = c // per_g
        prepare(c, 0)
        inside = head_loop_forward(c)
        cum_c = cum_p[c]

        @pl.when(me > 0)
        def _():
            forward_copy(c).wait_recv()

        @pl.when(me == 0)
        def _():
            f_recv[c] = jnp.zeros((STATE, CHUNK), BF16)

        held = f_recv[c]
        decay = jnp.exp(cum_c[T - 1 : T])
        f_send[c] = (decay * held.astype(F32) + added[:, at]).astype(BF16)

        @pl.when(me < n_ctx - 1)
        def _():
            forward_copy(c).start()

        readout = dot(bcc[1, g], held)
        own = inside + jnp.exp(cum_c) * readout
        x_f = xc[:, at].astype(F32)
        total = own + expand(c) * x_f
        mixed[:, at] = total
        gate = gate_ref[:, at].astype(F32)
        gated = total * (gate * sigmoid(gate))
        upstream = go_ref[:, at].astype(F32) * gain_ref[:, at]
        acc_sq[...] += gated * gated
        acc_proj[...] += upstream * gated
        return carry

    lax.fori_loop(0, chunks, forward, 0)

    ones = jnp.ones((8, CHUNK), F32)
    stats[mh, 0:8, :] = dot(ones, acc_sq[...], ca=1, cb=1, precision=HIGH)
    stats[mh, 8:16, :] = dot(ones, acc_proj[...], ca=1, cb=1, precision=HIGH)

    def stat_copy(k):
        return remote(
            stats.at[mh], stats.at[mh], st_s.at[k], st_r.at[k], head=lax.rem(mh + k, n_head)
        )

    for k in range(1, n_head):
        stat_copy(k).start()
    for k in range(1, n_head):
        source = lax.rem(mh + n_head - k, n_head)
        remote(stats.at[source], stats.at[source], st_s.at[k], st_r.at[k], head=source).wait_recv()
    for k in range(1, n_head):
        stat_copy(k).wait_send()
    total_stats = stats[0]
    for k in range(1, n_head):
        total_stats = total_stats + stats[k]
    eighth = jnp.full((8, CHUNK), 0.125, F32)
    square = dot(total_stats[0:8], eighth, ca=0, cb=0, precision=HIGH)
    raw_proj = dot(total_stats[8:16], eighth, ca=0, cb=0, precision=HIGH)
    factor = lax.rsqrt(square / INNER + epsilon)
    acc_sq[...] = factor
    acc_proj[...] = raw_proj * factor / INNER

    dtap[0:8, :] = jnp.zeros((8, CHUNK), F32)
    dtap[8 + T : 16 + T, :] = jnp.zeros((8, CHUNK), F32)

    def conv_back(lanes, d_pre, w):
        dtap[8 : 8 + T, 0:lanes] = d_pre
        total = w[0:1] * dtap[pl.ds(3, T + 8), 0:lanes]
        for k in range(1, CONV):
            total = total + w[k : k + 1] * dtap[pl.ds(3 - k, T + 8), 0:lanes]
        taps = [
            jnp.sum(d_pre * tap[pl.ds(5 + k, T), 0:lanes], axis=0, keepdims=True)
            for k in range(CONV)
        ]
        return total, taps

    def silu_slope(v):
        s = sigmoid(v)
        return s * (1.0 + v * (1.0 - s))

    def gate_back(c, carry):
        at = span(c)
        g = c // per_g
        total = mixed[:, at]
        gate = gate_ref[:, at].astype(F32)
        sig = sigmoid(gate)
        act = gate * sig
        factor_c = acc_sq[...]
        go = go_ref[:, at].astype(F32)
        normed = total * act * factor_c
        d_gated = (go * gain_ref[:, at] - normed * acc_proj[...]) * factor_c
        part[4:5, at] = jnp.sum(go * normed, axis=0, keepdims=True)
        ggate_ref[:, at] = (d_gated * total * (sig * (1.0 + gate * (1.0 - sig)))).astype(BF16)
        dy = d_gated * act
        d_mixed[:, at] = dy
        cum_c = cum_p[c]
        dye = (dy * jnp.exp(cum_c)).astype(BF16)
        d_enter = dot(c_t[g], dye).astype(BF16).astype(F32)

        @pl.when(me < n_ctx - 1)
        def _():
            reverse_copy(c).wait_recv()

        @pl.when(me == n_ctx - 1)
        def _():
            r_recv[c] = jnp.zeros((STATE, CHUNK), BF16)

        after = r_recv[c]
        after_f = after.astype(F32)
        decay = jnp.exp(cum_c[T - 1 : T])
        r_send[c] = (d_enter + decay * after_f).astype(BF16)

        @pl.when(me > 0)
        def _():
            reverse_copy(c).start()

        held = f_recv[c]
        d_c[g] += dot(dye, held, ca=1, cb=1)
        x_low = xc[:, at]
        x_f = x_low.astype(F32)
        d_scaled = dot(bcc[0, g], after).astype(BF16).astype(F32)
        d_b[g] += dot(scaled[:, at], after, ca=1, cb=1)
        d_w = d_scaled * jnp.exp(cum_c[T - 1 : T] - cum_c) * step_p[c]
        dx_parts = []
        d_score = d_s[g]
        for pair in range(HPC // 2):
            ln = slice(pair * 128, pair * 128 + 128)
            x_pair = x_low[:, ln]
            dy_pair = dy[:, ln]
            dy_low = dy_pair.astype(BF16)
            zero = jnp.zeros((T, 128), F32)
            ds = []
            for q in range(2):
                h = c * HPC + pair * 2 + q
                own = jnp.where(half, dy_pair, zero) if q == 0 else jnp.where(half, zero, dy_pair)
                d_mix = dot(own.astype(BF16), x_pair, ca=1, cb=1).astype(BF16).astype(F32)
                d_score = d_score + d_mix * weight[h]
                ds.append(dot(mix[h], dy_low, ca=0, cb=0))
            dx_parts.append(jnp.where(half, ds[0], ds[1]))
        d_s[g] = d_score
        dx1 = jnp.concatenate(dx_parts, axis=1)
        skip = expand(c)
        both = dx1 + d_w
        q2 = x_f * both
        q1 = dy * (total - skip * x_f) - q2
        sel = selector(c)
        sel_low = sel.astype(BF16)
        acc1[...] += split_dot(q1, sel_low)
        acc2[...] += split_dot(q2, sel_low)
        last_row = jnp.sum(d_w * x_f, axis=0, keepdims=True) + decay * jnp.sum(
            after_f * held.astype(F32), axis=0, keepdims=True
        )
        skip_row = jnp.sum(dy * x_f, axis=0, keepdims=True)
        which = lax.broadcasted_iota(jnp.int32, (8, CHUNK), 0)
        two = jnp.where(which == 0, last_row, jnp.where(which == 1, skip_row, 0.0))
        acc_row[...] += dot(two, sel, precision=HIGH)

        d_x = (both + skip * dy).astype(BF16).astype(F32)
        d_pre = d_x * silu_slope(pre_x[:, at])
        tap[0:8, :] = halo_x[:, at].astype(F32)[8:16]
        tap[8 : 8 + T, :] = x_ref[:, at].astype(F32)
        full, taps = conv_back(CHUNK, d_pre, wx_ref[:, at])
        for k in range(CONV):
            part[k : k + 1, at] = taps[k]
        border_send[:, at] = full[0:8]
        gx_ref[:, at] = full[8:].astype(BF16)
        tail_x[:, at] = full[T - 8 :]
        return carry

    lax.fori_loop(0, chunks, gate_back, 0)

    for g in range(groups):
        d_low = d_s[g].astype(BF16)
        d_c[g] += dot(d_low, bcc[0, g])
        d_b[g] += dot(d_low, bcc[1, g], ca=0, cb=0)
    for kind in range(2):
        for g in range(groups):
            at = slice(g * STATE, (g + 1) * STATE)
            out_at = slice(kind * columns + g * STATE, kind * columns + (g + 1) * STATE)
            grad = (d_b if kind == 0 else d_c)[g].astype(BF16).astype(F32)
            d_pre = grad * silu_slope(pre_bc[kind, g])
            tap[0:8, 0:STATE] = halo_bc[kind, :, at].astype(F32)[8:16]
            tap[8 : 8 + T, 0:STATE] = bc_ref[kind, :, at].astype(F32)
            full, taps = conv_back(STATE, d_pre, wbc_ref[kind, :, at])
            for k in range(CONV):
                part[8 + k : 9 + k, out_at] = taps[k]
            border_send[:, width + kind * columns + g * STATE : width + kind * columns + (g + 1) * STATE] = full[0:8]
            gbc_ref[kind, :, at] = full[8:].astype(BF16)
            tail_bc[kind, :, at] = full[T - 8 :]

    border = remote(border_send, border_recv, bo_s.at[0], bo_r.at[0], ctx=prv)

    @pl.when(me > 0)
    def _():
        border.start()

    is_last = lax.broadcasted_iota(jnp.int32, (T, heads), 0) == T - 1
    d_cum = acc1[...] + jnp.where(is_last, acc_row[0:1, :], 0.0)
    d_log = dot(lower, d_cum, ca=0, cb=0, precision=HIGH)
    shifted = logits_ref[...] + params_ref[0:1, :]
    step = jnp.maximum(shifted, 0.0) + jnp.log1p(jnp.exp(-jnp.abs(shifted)))
    rate = -jnp.exp(params_ref[1:2, :])
    d_step = acc2[...] / step + d_log * rate
    d_logit = d_step * sigmoid(shifted)
    gstep_ref[...] = d_logit
    part[12:13, 0:heads] = jnp.sum(d_logit, axis=0, keepdims=True)
    part[13:14, 0:heads] = jnp.sum(d_log * step, axis=0, keepdims=True) * rate
    part[14:15, 0:heads] = acc_row[1:2, :]

    totals[me] = part[...].astype(BF16)

    def total_copy(k):
        return remote(
            totals.at[me], totals.at[me], to_s.at[k], to_r.at[k], ctx=lax.rem(me + k, n_ctx)
        )

    for k in range(1, n_ctx):
        total_copy(k).start()

    @pl.when(me < n_ctx - 1)
    def _():
        border.wait_recv()
        pad = jnp.zeros((8, width), F32)
        gx_ref[T - 16 : T, :] = (
            tail_x[...] + jnp.concatenate([pad, border_recv[:, 0:width]], axis=0)
        ).astype(BF16)
        for kind in range(2):
            pad2 = jnp.zeros((8, columns), F32)
            got = border_recv[:, width + kind * columns : width + (kind + 1) * columns]
            gbc_ref[kind, T - 16 : T, :] = (
                tail_bc[kind] + jnp.concatenate([pad2, got], axis=0)
            ).astype(BF16)

    for k in range(1, n_ctx):
        source = lax.rem(me + n_ctx - k, n_ctx)
        remote(totals.at[source], totals.at[source], to_s.at[k], to_r.at[k], ctx=source).wait_recv()
    whole = totals[0].astype(F32)
    for k in range(1, n_ctx):
        whole = whole + totals[k].astype(F32)
    gwx_ref[...] = whole[0:4]
    ggain_ref[...] = whole[4:5]
    for kind in range(2):
        gwbc_ref[kind] = whole[8:12, kind * columns : (kind + 1) * columns]
    gparams_ref[...] = whole[12:15, 0:heads]

    for k in range(1, n_ctx):
        total_copy(k).wait_send()

    @pl.when(me > 0)
    def _():
        border.wait_send()

    def drain(c, carry):
        @pl.when(me < n_ctx - 1)
        def _():
            forward_copy(c).wait_send()

        @pl.when(me > 0)
        def _():
            reverse_copy(c).wait_send()

        return carry

    lax.fori_loop(0, chunks, drain, 0)


def shards(n_ctx, n_head, x, bc, gate, logits, wx, wbc, params, gain, go):
    T, width = x.shape
    columns = bc.shape[2]
    groups = columns // STATE
    heads = width // HEAD_DIM
    chunks = width // CHUNK
    V = pltpu.VMEM
    D = pltpu.SemaphoreType.DMA
    out_shape = (
        jax.ShapeDtypeStruct(x.shape, BF16),
        jax.ShapeDtypeStruct(bc.shape, BF16),
        jax.ShapeDtypeStruct(x.shape, BF16),
        jax.ShapeDtypeStruct(logits.shape, F32),
        jax.ShapeDtypeStruct(wx.shape, F32),
        jax.ShapeDtypeStruct(wbc.shape, F32),
        jax.ShapeDtypeStruct(params.shape, F32),
        jax.ShapeDtypeStruct((1, width), F32),
    )
    scratch = [
        V((16, width), BF16), V((2, 16, columns), BF16),
        V((heads, T, 128), F32), V((chunks, T, CHUNK), F32), V((chunks, T, CHUNK), F32),
        V((heads, T), F32), V((heads, T), F32), V((T, T), F32),
        V((T + 8, CHUNK), F32), V((T + 16, CHUNK), F32),
        V((T, width), BF16), V((T, width), F32),
        V((2, groups, T, STATE), BF16), V((2, groups, T, STATE), F32),
        V((groups, STATE, T), BF16), V((groups, STATE, T), BF16), V((groups, T, T), F32),
        V((heads, T, T), BF16), V((heads, T, T), F32),
        V((T, width), BF16), V((STATE, width), F32),
        V((chunks, STATE, CHUNK), BF16), V((chunks, STATE, CHUNK), BF16),
        V((chunks, STATE, CHUNK), BF16), V((chunks, STATE, CHUNK), BF16),
        V((T, width), F32), V((T, width), F32),
        V((T, CHUNK), F32), V((T, CHUNK), F32), V((n_head, 16, T), F32),
        V((groups, T, STATE), F32), V((groups, T, STATE), F32), V((groups, T, T), F32),
        V((T, heads), F32), V((T, heads), F32), V((8, heads), F32),
        V((8, width + 2 * columns), F32), V((8, width + 2 * columns), F32),
        V((16, width), F32), V((2, 16, columns), F32),
        V((16, width), F32), V((n_ctx, 16, width), BF16),
        D((2,)), D((2,)),
        D((chunks,)), D((chunks,)), D((chunks,)), D((chunks,)),
        D((n_head,)), D((n_head,)), D((1,)), D((1,)), D((n_ctx,)), D((n_ctx,)),
    ]
    outs = pl.pallas_call(
        functools.partial(kernel, n_ctx, n_head),
        out_shape=out_shape,
        in_specs=[pl.BlockSpec(memory_space=pltpu.VMEM)] * 9,
        out_specs=tuple([pl.BlockSpec(memory_space=pltpu.VMEM)] * 8),
        scratch_shapes=scratch,
        compiler_params=pltpu.CompilerParams(
            collective_id=0, has_side_effects=True, vmem_limit_bytes=60 * 1024 * 1024
        ),
        name="mixer_step",
    )(x, bc, gate, logits, wx, wbc, params, gain.reshape(1, width), go)
    return outs[:7] + (outs[7].reshape(width),)


def solution(mesh):
    return jax.shard_map(
        functools.partial(shards, mesh.shape["ctx"], mesh.shape["head"]),
        mesh=mesh,
        in_specs=(
            P(("group", "ctx"), "head"),
            P(None, ("group", "ctx"), "head"),
            P(("group", "ctx"), "head"),
            P(("group", "ctx"), "head"),
            P(None, "head"),
            P(None, None, "head"),
            P(None, "head"),
            P("head"),
            P(("group", "ctx"), "head"),
        ),
        out_specs=(
            P(("group", "ctx"), "head"),
            P(None, ("group", "ctx"), "head"),
            P(("group", "ctx"), "head"),
            P(("group", "ctx"), "head"),
            P("group", "head"),
            P("group", None, "head"),
            P("group", "head"),
            P(("group", "head")),
        ),
        check_vma=False,
    )
```

time: 252 us -> 83.3 us (0.33)
  Pallas kernels: 0 us -> 72.6 us
  other arithmetic: 70 us -> 0 us
  blocking collectives: 61 us -> 0 us
  waiting for transfers between devices: 32.5 us -> 0 us
  local copies, waits for them, and re-layouts: 41.1 us -> 9.74 us
  matrix products: 23.3 us -> 0 us
  between operations: 15.4 us -> 0.65 us
  starting transfers between devices: 6.37 us -> 0 us
    pallas_call x0 -> x1, Pallas kernels: none -> 72.6 us  [shards(): pl.pallas_call(functools.partial(kernel, n_ctx, n_head), out_shape=out_sh...]
    psum x3 -> x0, blocking collectives: 33.4 us -> none  [the longest x1 20.3 us: shards(): lax.psum((gradients[4], gradients[5], gradients[6], grad_gain_own), 'ctx')]
    all_gather x3 -> x0, waiting for transfers between devices: 32.4 us -> none  [the longest x2 25.6 us: entering_2(): lax.all_gather(part.astype(kind), axis)]
    all_gather x3 -> x0, blocking collectives: 27.5 us -> none  [the longest x2 17.6 us: entering_2(): lax.all_gather(part.astype(kind), axis)]
    dot_general x12 -> x0, matrix products: 23.3 us -> none  [the longest x3 14.3 us: span_parts(): jnp.einsum('gkts,sgkp->tgkp', mixing, x_block, preferred_element_type=jnp...]
    reduce_sum x11 -> x0, other arithmetic: 23.2 us -> none  [the longest x2 6.22 us: span_parts(): inside = inside + skip_gain[None, :, :, None] * x_block.astype(jnp.float32)]
    select_n x13 -> x0, other arithmetic: 14.8 us -> none  [the longest x8 8.73 us: entering_step(): return jax.tree.map(lambda a, b: jnp.where(reached, a, b), new, before)]
    convert_element_type x4 -> x0, other arithmetic: 8.31 us -> none  [the longest x2 8.12 us: conv_silu(): return jax.nn.silu(summed).astype(jnp.bfloat16)]
  transfers between devices with their start and end apart: 5 -> 0, of which waited for: 3 -> 0; matrix products, arithmetic and copies ran while one was open for 21% -> 0% of each run, Pallas kernels for 0% -> 0%
where the time goes in v1:
time: 83.3 us; the launch traced here: 83 us
  Pallas kernels  72.6 us (87%)
  local copies, waits for them, and re-layouts  9.74 us (12%)
    pallas_call x1, Pallas kernels, shards(): pl.pallas_call(functools.partial(kernel, n_ctx, n_head), out_shape=out_sh...  72.6 us
    unnamed x21, local copies, waits for them, and re-layouts  9.74 us

profile of v1, /device:TPU:0, one launch (start us, length us, event | category | flops | bytes accessed | tf_op | source)
XLA Modules:
  0.0 83.0 jit_solution(16771506213610738999)
XLA Ops:
  0.6 1.5 %copy.17.logits_ref = f32[256,32]{1,0:T(8,128)} copy(f32[256,32]{0,1:T(8,128)} %param.12) | data formatting | bytes 65536 | tf_op args[3]
  2.1 72.6 %mixer_step.1 = (bf16[256,2048]{1,0:T(8,128)(2,1)}, bf16[2,256,256]{2,1,0:T(8,128)(2,1)}, bf16[256,2048]{1,0:T(8,128)(2,1)}, f32[256,32]{1,0:T(8,128)}, f32[4,20...) custom-call(bf16[256,2048]{1,0:T(8,128)(2,1)} %x_ref.1, bf16[2,256,256]{2,1,0:T(8,128)(2,1)} %bc_ref.1, ...), custom_call_target="tpu_custom_call" | custom-call | tf_op jit(solution)/shard_map/mixer_step/pallas_call | solution.py:519
  74.8 1.6 %copy.18 = f32[256,32]{0,1:T(8,128)} copy(f32[256,32]{1,0:T(8,128)} %get-tuple-element.27) | data formatting | bytes 65536
  76.4 0.0 copy-start.1
  76.4 0.0 copy-start
  76.4 2.4 %copy.26 = bf16[256,2048]{1,0:T(8,128)(2,1)} copy(bf16[256,2048]{1,0:T(8,128)(2,1)} %get-tuple-element.40) | data formatting | bytes 2097152
  78.8 0.0 copy-done.1
  78.8 0.7 copy.27
  79.5 0.0 copy-done
  79.5 0.0 copy-start.2
  79.5 1.0 %copy.28 = bf16[256,2048]{1,0:T(8,128)(2,1)} copy(bf16[256,2048]{1,0:T(8,128)(2,1)S(1)} %copy-done) | data formatting | bytes 2097152
  80.5 0.0 copy-done.2
  80.5 0.0 copy-start.4
  80.5 0.6 copy.29
  81.1 0.1 copy-done.4
  81.2 0.0 copy-start.5
  81.2 0.0 copy-start.3
  81.2 0.6 copy.30
  81.8 0.1 copy-done.5
  81.8 0.6 copy.31
  82.4 0.0 copy-done.3
  82.4 0.6 copy.32
Async XLA Ops:
  76.4 2.4 %copy-start.1 = (bf16[2,256,256]{2,1,0:T(8,128)(2,1)S(1)}, bf16[2,256,256]{2,1,0:T(8,128)(2,1)}, u32[]{:S(2)}) copy-start(bf16[2,256,256]{2,1,0:T(8,128)(2,1)} %get-tuple-element.41) | copy-start | bytes 786436
  76.4 3.1 %copy-start = (bf16[256,2048]{1,0:T(8,128)(2,1)S(1)}, bf16[256,2048]{1,0:T(8,128)(2,1)}, u32[]{:S(2)}) copy-start(bf16[256,2048]{1,0:T(8,128)(2,1)} %get-tuple-element.42) | copy-start | bytes 3145732
  79.5 1.0 %copy-start.2 = (f32[4,2048]{1,0:T(4,128)S(1)}, f32[4,2048]{1,0:T(4,128)}, u32[]{:S(2)}) copy-start(f32[4,2048]{1,0:T(4,128)} %get-tuple-element.44) | copy-start | bytes 98308
  80.5 0.7 copy-start.4
  81.2 0.7 copy-start.5
  81.2 1.2 %copy-start.3 = (f32[1,2048]{1,0:T(1,128)S(1)}, f32[1,2048]{1,0:T(1,128)}, u32[]{:S(2)}) copy-start(f32[1,2048]{1,0:T(1,128)} %get-tuple-element.23) | copy-start | bytes 24580
